TPU v7x, 32 devices: a whole 2x2x4 slice. The times are simulated.
32 devices in a mesh: seq: 8 (over z, x), tp: 4 (over y, core).
Axes of the slice: x: 2, y: 2, z: 4, core: 2. Of those that a mesh axis runs over, the one named last changes fastest.
Arguments:
- query_heads: bfloat16 [2048, 2048], P('seq', 'tp'), may hold values from -96 to 96
- key_heads: bfloat16 [2048, 2048], P('seq', 'tp'), may hold values from -4 to 4
- value_heads: bfloat16 [2048, 2048], P('seq', 'tp'), may hold values from -6 to 6
- residual: bfloat16 [2048, 4096], P('seq'), may hold values from -64 to 64
- out_weight: bfloat16 [2048, 4096], P('tp'), may hold values from -0.125 to 0.125
- ln_gain: float32 [4096], replicated, may hold values from 0.1 to 1.9
- up_source: bfloat16 [4096, 4096], P(None, 'tp'), may hold values from -0.09375 to 0.09375
- down_source: bfloat16 [4096, 4096], P('tp'), may hold values from -0.09375 to 0.09375
- copy_gain: float32 [4096], P('tp'), may hold values from 0.3 to 3
- neuron_source: int32 [4096], P('tp'), may hold values from 0 to 4095, as said below
- cotangent: bfloat16 [2048, 4096], P('seq'), may hold values from -6 to 6
Outputs:
- encoded: float32 [2048, 4096], P(('seq', 'tp'))
- grad_query: float32 [2048, 2048], P('seq', 'tp')
- grad_key: float32 [2048, 2048], P('seq', 'tp')
- grad_value: float32 [2048, 2048], P('seq', 'tp')
- grad_residual: float32 [2048, 4096], P('seq', 'tp')
Inputs may be any that keep to these rules, and one draw needn't show every extreme that they name: Added neuron j splits a source neuron of its own group: neuron_source[j] // 1024 == j // 1024.
All inputs are finite; a program needn't handle non-finite values.
Results may differ from a plain program's by a relative error of at most 0.035.
Values may be sent and summed in bfloat16 or wider, within the bound.
A program may use at most 128 MiB of HBM per device.

v0:
```python
import math
import jax
import jax.numpy as jnp
from jax import lax
from jax.sharding import PartitionSpec as P

HEAD_DIM = 128
epsilon = 1e-05


def from_behind(array, axis, by):
    count = lax.axis_size(axis)
    pairs = [(i, i + by) for i in range(count) if 0 <= i + by < count]
    return lax.ppermute(array, axis, pairs)


def gelu_slope(inputs):
    output, pull_back = jax.vjp(jax.nn.gelu, inputs)
    return (output, pull_back(jnp.ones_like(inputs))[0])


def layer_norm_rows(stream):
    centered = stream - jnp.mean(stream, axis=-1, keepdims=True)
    row_sigma = jnp.sqrt(jnp.mean(centered * centered, axis=-1, keepdims=True) + epsilon)
    return (centered / row_sigma, row_sigma)


def bfloat16_term(values):
    return lax.optimization_barrier(values.astype(jnp.bfloat16)).astype(jnp.float32)


def shards(
    query_heads,
    key_heads,
    value_heads,
    residual,
    out_weight,
    ln_gain,
    up_source,
    down_source,
    copy_gain,
    neuron_source,
    cotangent,
):
    tok_rows = query_heads.shape[0]
    head_width = query_heads.shape[1]
    head_count = head_width // HEAD_DIM
    model_width = residual.shape[1]
    score_scale = 1.0 / math.sqrt(HEAD_DIM)
    cycle_place = lax.axis_index("seq")
    blocks = lax.axis_size("seq")
    tp_place = lax.axis_index("tp")
    groups = lax.axis_size("tp")
    kv_pair = jnp.stack([key_heads, value_heads])
    kv_blocks = {0: kv_pair}
    for offset in (-2, -1, 1, 2):
        kv_blocks[offset] = from_behind(kv_pair, "seq", -offset)
    window = jnp.concatenate([kv_blocks[offset] for offset in (-2, -1, 0, 1, 2)], axis=1)
    keys_all = window[0].reshape(5 * tok_rows, head_count, HEAD_DIM)
    values_all = window[1].reshape(5 * tok_rows, head_count, HEAD_DIM)
    block_of = jnp.arange(5 * tok_rows, dtype=jnp.int32) // tok_rows - 2 + cycle_place
    is_valid = (block_of >= 0) & (block_of < blocks)
    queries = query_heads.reshape(tok_rows, head_count, HEAD_DIM)
    scores = (
        jnp.einsum("rhd,khd->hrk", queries, keys_all, preferred_element_type=jnp.float32)
        * score_scale
    )
    scores = jnp.where(is_valid[None, None, :], scores, -jnp.inf)
    row_top = jnp.max(scores, axis=-1, keepdims=True)
    exp_scores = jnp.exp(scores - row_top)
    attn_probs = exp_scores / jnp.sum(exp_scores, axis=-1, keepdims=True)
    attn_low = attn_probs.astype(jnp.bfloat16)
    attended = jnp.einsum(
        "hrk,khd->rhd", attn_low, values_all, preferred_element_type=jnp.float32
    ).astype(jnp.bfloat16)
    attended = attended.reshape(tok_rows, head_width)
    head_part = bfloat16_term(jnp.dot(attended, out_weight, preferred_element_type=jnp.float32))
    head_mix = lax.psum(head_part.astype(jnp.bfloat16), "tp").astype(jnp.float32)
    stream = residual.astype(jnp.float32) + head_mix
    unit_rows, row_sigma = layer_norm_rows(stream)
    normed_full = unit_rows * ln_gain
    normed = normed_full.astype(jnp.bfloat16)
    src_width = up_source.shape[1]
    local_source = neuron_source - tp_place * src_width
    pick = (
        lax.broadcasted_iota(jnp.int32, (src_width, local_source.shape[0]), 0)
        == local_source[None, :]
    )
    counts = 1.0 + jnp.sum(pick.astype(jnp.float32), axis=1)
    pick = pick.astype(jnp.bfloat16)

    def copies_of(values):
        return jnp.dot(values.astype(jnp.bfloat16), pick, preferred_element_type=jnp.float32)

    def summed(values):
        return lax.dot_general(
            values.astype(jnp.bfloat16),
            pick,
            (((1,), (1,)), ((), ())),
            preferred_element_type=jnp.float32,
        )

    hidden_in = jnp.dot(normed, up_source, preferred_element_type=jnp.float32)
    copies_in = copies_of(hidden_in) * copy_gain
    act_src, slope_src = gelu_slope(hidden_in)
    act_copy, slope_copy = gelu_slope(copies_in)
    merged = ((act_src + summed(act_copy)) / counts).astype(jnp.bfloat16)
    owner_rows = tok_rows // groups
    ffn_out = lax.psum_scatter(
        bfloat16_term(jnp.dot(merged, down_source, preferred_element_type=jnp.float32)).astype(
            jnp.bfloat16
        ),
        "tp",
        scatter_dimension=0,
        tiled=True,
    ).astype(jnp.float32)
    own_normed = lax.dynamic_slice_in_dim(normed_full, tp_place * owner_rows, owner_rows, 0)
    encoded = own_normed + ffn_out
    grad_merged = lax.dot_general(
        cotangent, down_source, (((1,), (1,)), ((), ())), preferred_element_type=jnp.float32
    )
    inverse = 1.0 / counts
    grad_src = grad_merged * inverse * slope_src
    grad_copy = copies_of(grad_merged * inverse) * slope_copy
    grad_hidden = (grad_src + summed(grad_copy * copy_gain)).astype(jnp.bfloat16)
    back_part = bfloat16_term(
        lax.dot_general(
            grad_hidden, up_source, (((1,), (1,)), ((), ())), preferred_element_type=jnp.float32
        )
    )
    grad_normed = cotangent.astype(jnp.float32) + lax.psum(
        back_part.astype(jnp.bfloat16), "tp"
    ).astype(jnp.float32)
    scaled = grad_normed * ln_gain
    grad_stream = (
        scaled
        - jnp.mean(scaled, axis=-1, keepdims=True)
        - unit_rows * jnp.mean(scaled * unit_rows, axis=-1, keepdims=True)
    ) / row_sigma
    grad_low = grad_stream.astype(jnp.bfloat16)
    col_width = model_width // groups
    grad_residual = lax.dynamic_slice_in_dim(grad_stream, tp_place * col_width, col_width, 1)
    grad_attended = lax.dot_general(
        grad_low, out_weight, (((1,), (1,)), ((), ())), preferred_element_type=jnp.float32
    ).astype(jnp.bfloat16)
    grad_heads = grad_attended.reshape(tok_rows, head_count, HEAD_DIM)
    attended_heads = attended.reshape(tok_rows, head_count, HEAD_DIM)
    row_delta = jnp.sum(
        grad_heads.astype(jnp.float32) * attended_heads.astype(jnp.float32), axis=-1
    ).T
    grad_probs = jnp.einsum(
        "rhd,khd->hrk", grad_heads, values_all, preferred_element_type=jnp.float32
    )
    grad_scores = (attn_probs * (grad_probs - row_delta[:, :, None])).astype(jnp.bfloat16)
    grad_query = score_scale * jnp.einsum(
        "hrk,khd->rhd", grad_scores, keys_all, preferred_element_type=jnp.float32
    )
    grad_query = grad_query.reshape(tok_rows, head_width)
    grad_keys = score_scale * jnp.einsum(
        "hrk,rhd->khd", grad_scores, queries, preferred_element_type=jnp.float32
    )
    grad_values = jnp.einsum(
        "hrk,rhd->khd", attn_low, grad_heads, preferred_element_type=jnp.float32
    )
    partial_value = jnp.stack(
        [grad_keys.reshape(5 * tok_rows, head_width), grad_values.reshape(5 * tok_rows, head_width)]
    )
    pieces = {}
    for offset in (-2, -1, 0, 1, 2):
        pieces[offset] = partial_value[:, (offset + 2) * tok_rows : (offset + 3) * tok_rows]
    grad_total = pieces[0]
    for offset in (-2, -1, 1, 2):
        grad_total = grad_total + from_behind(
            pieces[offset].astype(jnp.bfloat16), "seq", offset
        ).astype(jnp.float32)
    grad_key = grad_total[0]
    grad_value = grad_total[1]
    return (encoded, grad_query, grad_key, grad_value, grad_residual)


def solution(mesh):
    in_specs = (
        P("seq", "tp"),
        P("seq", "tp"),
        P("seq", "tp"),
        P("seq", None),
        P("tp", None),
        P(),
        P(None, "tp"),
        P("tp", None),
        P("tp"),
        P("tp"),
        P("seq", None),
    )
    out_specs = (
        P(("seq", "tp"), None),
        P("seq", "tp"),
        P("seq", "tp"),
        P("seq", "tp"),
        P("seq", "tp"),
    )
    return jax.shard_map(shards, mesh=mesh, in_specs=in_specs, out_specs=out_specs, check_vma=False)
```

profile of v0, /device:TPU:16, one launch (start us, length us, event | category | flops | bytes accessed | tf_op | source)
XLA Modules:
  0.0 267.4 jit_solution(15022565528632856)
XLA Ops:
  7.2 1.1 copy.47
  8.3 1.1 copy.48
  9.4 3.5 %collective-permute-start = (bf16[2,256,512]{1,2,0:T(8,128)(2,1)S(1)}, bf16[2,256,512]{1,2,0:T(8,128)(2,1)S(1)}, u32[]{:S(2)}, u32[]{:S(2)}) collective-permute-start(bf16[2,256,512]{1,2,0:T(8,128)(2,1)S(1)} %pad_maximum_fusion.1), channel_id=1, source_target_pairs={{0,8},{4,12},{8,16},{12,20},{16,24},{20,28},{1,9},{5,13},{9,17},{1... | collective-permute-start | bytes 1572872 | tf_op jit(solution)/shard_map/ppermute | solution.py:14
  12.9 3.4 %collective-permute-start.1 = (bf16[2,256,512]{1,2,0:T(8,128)(2,1)S(1)}, bf16[2,256,512]{1,2,0:T(8,128)(2,1)S(1)}, u32[]{:S(2)}, u32[]{:S(2)}) collective-permute-start(bf16[2,256,512]{1,2,0:T(8,128)(2,1)S(1)} %pad_maximum_fusion.1), channel_id=1, source_target_pairs={{0,4},{4,8},{8,12},{12,16},{16,20},{20,24},{24,28},{1,5},{5,9},{9,... | collective-permute-start | bytes 1572872 | tf_op jit(solution)/shard_map/ppermute | solution.py:14
  16.3 2.4 collective-permute-start.3
  18.7 3.3 %collective-permute-start.2 = (bf16[2,256,512]{1,2,0:T(8,128)(2,1)S(1)}, bf16[2,256,512]{1,2,0:T(8,128)(2,1)S(1)}, u32[]{:S(2)}, u32[]{:S(2)}) collective-permute-start(bf16[2,256,512]{1,2,0:T(8,128)(2,1)S(1)} %pad_maximum_fusion.1), channel_id=1, source_target_pairs={{4,0},{8,4},{12,8},{16,12},{20,16},{24,20},{28,24},{5,1},{9,5},{13... | collective-permute-start | bytes 1572872 | tf_op jit(solution)/shard_map/ppermute | solution.py:14
  22.8 1.1 copy.71
  23.9 1.1 collective-permute-done
  25.0 12.2 %collective-permute-done.1 = bf16[2,256,512]{1,2,0:T(8,128)(2,1)S(1)} collective-permute-done((bf16[2,256,512]{1,2,0:T(8,128)(2,1)S(1)}, bf16[2,256,512]{1,2,0:T(8,128)(2,1)S(1)}, u32[]{:S(2)}, u32[]{:S(2)}) %collective-permute-start.1) | collective-permute-done | bytes 524320 | tf_op jit(solution)/shard_map/ppermute | solution.py:14
  37.4 7.3 %collective-permute-done.2 = bf16[2,256,512]{1,2,0:T(8,128)(2,1)S(1)} collective-permute-done((bf16[2,256,512]{1,2,0:T(8,128)(2,1)S(1)}, bf16[2,256,512]{1,2,0:T(8,128)(2,1)S(1)}, u32[]{:S(2)}, u32[]{:S(2)}) %collective-permute-start.2) | collective-permute-done | bytes 524320 | tf_op jit(solution)/shard_map/ppermute | solution.py:14
  45.0 4.2 %exponential_reduce_fusion = (f32[4,256]{1,0:T(4,128)S(1)}, f32[4,256,1280]{1,2,0:T(8,128)}) fusion(bf16[1280,4,128]{0,2,1:T(8,128)(2,1)S(1)} %bitcast.56, bf16[256,4,128]{0,2,1:T(8,128)(2,1)S(1)} %bitcast.66, pred[1280]{0:T(1024)(128)(4,1)S(1)} %fusion.80), kind=kOutput, calls=%fused_computation.14 | convolution fusion | flops 340788480 | bytes 6821120 | tf_op jit(solution)/shard_map/sub | solution.py:70
  49.2 4.0 %fusion.20 = bf16[4,256,1280]{1,2,0:T(8,128)(2,1)S(1)} fusion(f32[4,256]{1,0:T(4,128)S(1)} %get-tuple-element.32, f32[4,256,1280]{1,2,0:T(8,128)} %get-tuple-element.33), kind=kLoop, calls=%fused_computation.40 | loop fusion | flops 2621440 | bytes 7868416 | tf_op jit(solution)/shard_map/convert_element_type | solution.py:72
  53.2 1.5 copy-done.3
  55.2 2.7 %convolution_convert_fusion.2 = bf16[256,4096]{1,0:T(8,128)(2,1)} fusion(bf16[256,512]{0,1:T(8,128)(2,1)S(1)} %bitcast.58, bf16[512,4096]{1,0:T(8,128)(2,1)S(1)} %copy-done.6), kind=kOutput, calls=%fused_computation.12 | convolution fusion | flops 1074790400 | bytes 6553600 | tf_op jit(solution)/shard_map/dot_general | solution.py:77
  58.7 7.5 %convolution_multiply_fusion.1 = f32[256,1024]{1,0:T(8,128)} fusion(bf16[256,4096]{1,0:T(8,128)(2,1)} %param.21, bf16[1024,4096]{1,0:T(8,128)(2,1)} %param.18, f32[1024]{0:T(1024)S(1)} %get-tuple-element.30), kind=kOutput, calls=%fused_computation.50 | convolution fusion | flops 2147745792 | bytes 11538432 | tf_op jit(solution)/shard_map/dot_general | solution.py:119
  66.2 43.4 %all-reduce.3.cloned.1.call-done = bf16[256,4096]{1,0:T(8,128)(2,1)} async-done(((bf16[256,4096]{1,0:T(8,128)(2,1)}), bf16[256,4096]{1,0:T(8,128)(2,1)}) %all-reduce.3.cloned.1.call-update) | async-done | bytes 2097168 | tf_op jit(solution)/shard_map/psum | solution.py:78
  109.7 2.4 fusion.9
  113.0 1.0 broadcast_multiply_fusion
  114.0 7.2 %fusion.18 = f32[256,1024]{1,0:T(8,128)S(1)} fusion(bf16[4096,1024]{1,0:T(8,128)(2,1)} %param.17, f32[256,4096]{1,0:T(8,128)S(1)} %broadcast_multiply_fusion), kind=kOutput, calls=%fused_computation.37 | convolution fusion | flops 2148532224 | bytes 13631488 | tf_op jit(solution)/shard_map/dot_general | solution.py:103
  122.2 2.0 fusion.21
  124.2 5.3 %fusion.26 = bf16[256,1024]{1,0:T(8,128)(2,1)S(1)} fusion(s32[1024]{0:T(1024)S(1)} %broadcast_subtract_fusion, f32[256,1024]{1,0:T(8,128)} %convolution_multiply_fusion.1, f32[256,1024]{1,0:T(8,128)} %copy-done.18, f32[256,1024]{1,0:T(8,128)} %fusion.21, f32[1024]{0:T(1024)S(1)} %copy-done.17), kind=kOutput, calls=%fused_computation.51 | convolution fusion | flops 1086586880 | bytes 3678208 | tf_op jit(solution)/shard_map/dot_general | solution.py:96
  129.5 7.3 %convolution_convert_fusion = bf16[256,4096]{1,0:T(8,128)(2,1)} fusion(bf16[256,1024]{1,0:T(8,128)(2,1)S(1)} %fusion.26, bf16[4096,1024]{1,0:T(8,128)(2,1)} %param.17), kind=kOutput, calls=%fused_computation.10 | convolution fusion | flops 2148532224 | bytes 11010048 | tf_op jit(solution)/shard_map/dot_general | solution.py:127
  136.9 9.1 %convolution_convert_fusion.1 = bf16[256,4096]{1,0:T(8,128)(2,1)} fusion(bf16[1024,4096]{1,0:T(8,128)(2,1)} %param.18, s32[1024]{0:T(1024)S(1)} %broadcast_subtract_fusion, f32[256,1024]{1,0:T(8,128)} %copy-done.18, f32[256,1024]{1,0:T(8,128)} %fusion.21, f32[1024]{0:T(1024)S(1)} %get-tuple-element.31), kind=kOutput, calls=%fused_computation.11 | convolution fusion | flops 2691694592 | bytes 12591104 | tf_op jit(solution)/shard_map/dot_general | solution.py:110
  146.1 42.4 %all-reduce.5.cloned.1.call-done = bf16[256,4096]{1,0:T(8,128)(2,1)} async-done(((bf16[256,4096]{1,0:T(8,128)(2,1)}), bf16[256,4096]{1,0:T(8,128)(2,1)}) %all-reduce.5.cloned.1.call-update) | async-done | bytes 2097168 | tf_op jit(solution)/shard_map/psum | solution.py:131
  188.5 4.3 %fusion.11 = (f32[256]{0:T(256)S(1)}, f32[256]{0:T(256)S(1)}) fusion(bf16[256,4096]{1,0:T(8,128)(2,1)} %all-reduce.5.cloned.1.call-done, bf16[256,4096]{1,0:T(8,128)(2,1)} %param.21, f32[4096]{0:T(1024)S(1)} %copy-done.16, f32[256]{0:T(256)S(1)} %add_sqrt_fusion, f32[256]{0:T(256)S(1)} %broadcast_multiply_fusion.3, ...), kind=kLoop, calls=%fused_computation.30 | loop fusion | flops 12582400 | bytes 8409088 | tf_op jit(solution)/shard_map/reduce_sum | solution.py:137
  193.2 2.4 subtract_divide_fusion
  195.6 2.1 copy-done.5
  197.7 1.3 fusion.30
  199.8 2.5 fusion.100
  202.3 2.1 copy.61
  204.5 4.2 %multiply_convert_fusion = bf16[4,256,1280]{1,2,0:T(8,128)(2,1)S(1)} fusion(bf16[256,4,128]{0,2,1:T(8,128)(2,1)S(1)} %bitcast.64, bf16[1280,4,128]{0,2,1:T(8,128)(2,1)} %bitcast.55, f32[4,256]{1,0:T(4,128)S(1)} %bitcast.68, f32[4,256]{1,0:T(4,128)S(1)} %get-tuple-element.32, f32[4,256,1280]{1,2,0:T(8,128)} %get-tuple-element.33), kind=kOutput, calls=%fused_computation.8 | convolution fusion | flops 340787200 | bytes 9445376 | tf_op jit(solution)/shard_map/rhd,khd->hrk/dot_general | solution.py:151
  208.7 1.5 copy-done.8
  210.2 2.5 convolution_multiply_fusion
  212.7 3.2 %copy.60 = f32[1,1280,512]{2,1,0:T(8,128)} copy(f32[1,1280,512]{1,2,0:T(8,128)} %bitcast.53) | data formatting | bytes 5242880 | tf_op jit(solution)/shard_map/stack;reshape | solution.py:165
  216.0 2.2 fusion.2
  218.2 1.4 fusion.98
  219.6 2.4 collective-permute-start.4
  222.0 4.2 %collective-permute-start.7 = (bf16[2,256,512]{2,1,0:T(8,128)(2,1)}, bf16[2,256,512]{2,1,0:T(8,128)(2,1)}, u32[]{:S(2)}, u32[]{:S(2)}) collective-permute-start(bf16[2,256,512]{2,1,0:T(8,128)(2,1)} %get-tuple-element.23), channel_id=1, source_target_pairs={{0,8},{4,12},{8,16},{12,20},{16,24},{20,28},{1,9},{5,13},{9,17},{1... | collective-permute-start | bytes 1572872 | tf_op jit(solution)/shard_map/ppermute | solution.py:14
  226.2 3.4 %collective-permute-start.6 = (bf16[2,256,512]{2,1,0:T(8,128)(2,1)}, bf16[2,256,512]{2,1,0:T(8,128)(2,1)}, u32[]{:S(2)}, u32[]{:S(2)}) collective-permute-start(bf16[2,256,512]{2,1,0:T(8,128)(2,1)} %get-tuple-element.24), channel_id=1, source_target_pairs={{0,4},{4,8},{8,12},{12,16},{16,20},{20,24},{24,28},{1,5},{5,9},{9,... | collective-permute-start | bytes 1572872 | tf_op jit(solution)/shard_map/ppermute | solution.py:14
  229.6 3.4 %collective-permute-start.5 = (bf16[2,256,512]{2,1,0:T(8,128)(2,1)}, bf16[2,256,512]{2,1,0:T(8,128)(2,1)}, u32[]{:S(2)}, u32[]{:S(2)}) collective-permute-start(bf16[2,256,512]{2,1,0:T(8,128)(2,1)} %get-tuple-element.25), channel_id=1, source_target_pairs={{4,0},{8,4},{12,8},{16,12},{20,16},{24,20},{28,24},{5,1},{9,5},{13... | collective-permute-start | bytes 1572872 | tf_op jit(solution)/shard_map/ppermute | solution.py:14
  233.0 2.7 convolution_multiply_fusion.2
  235.6 1.0 copy.62
  236.6 2.3 constant_dynamic-slice_fusion
  238.9 12.3 %collective-permute-done.6 = bf16[2,256,512]{2,1,0:T(8,128)(2,1)} collective-permute-done((bf16[2,256,512]{2,1,0:T(8,128)(2,1)}, bf16[2,256,512]{2,1,0:T(8,128)(2,1)}, u32[]{:S(2)}, u32[]{:S(2)}) %collective-permute-start.6) | collective-permute-done | bytes 524320 | tf_op jit(solution)/shard_map/ppermute | solution.py:14
  251.2 4.1 %collective-permute-done.5 = bf16[2,256,512]{2,1,0:T(8,128)(2,1)} collective-permute-done((bf16[2,256,512]{2,1,0:T(8,128)(2,1)}, bf16[2,256,512]{2,1,0:T(8,128)(2,1)}, u32[]{:S(2)}, u32[]{:S(2)}) %collective-permute-start.5) | collective-permute-done | bytes 524320 | tf_op jit(solution)/shard_map/ppermute | solution.py:14
  255.4 2.0 fusion.50
  257.4 1.0 slice_bitcast_fusion
  258.4 2.4 convert_add_fusion.1
  (63 shorter events, 5.8 us)
Async XLA Ops:
  7.2 102.5 %all-reduce.3.cloned.1.call-start = ((), (), s32[]{:S(2)}) async-start(), calls=%async_computation.1 | async-start | bytes 4194304 | tf_op jit(solution)/shard_map/psum | solution.py:78
  9.4 15.6 %collective-permute-start = (bf16[2,256,512]{1,2,0:T(8,128)(2,1)S(1)}, bf16[2,256,512]{1,2,0:T(8,128)(2,1)S(1)}, u32[]{:S(2)}, u32[]{:S(2)}) collective-permute-start(bf16[2,256,512]{1,2,0:T(8,128)(2,1)S(1)} %pad_maximum_fusion.1), channel_id=1, source_target_pairs={{0,8},{4,12},{8,16},{12,20},{16,24},{20,28},{1,9},{5,13},{9,17},{1... | collective-permute-start | bytes 1572872 | tf_op jit(solution)/shard_map/ppermute | solution.py:14
  12.9 24.3 %collective-permute-start.1 = (bf16[2,256,512]{1,2,0:T(8,128)(2,1)S(1)}, bf16[2,256,512]{1,2,0:T(8,128)(2,1)S(1)}, u32[]{:S(2)}, u32[]{:S(2)}) collective-permute-start(bf16[2,256,512]{1,2,0:T(8,128)(2,1)S(1)} %pad_maximum_fusion.1), channel_id=1, source_target_pairs={{0,4},{4,8},{8,12},{12,16},{16,20},{20,24},{24,28},{1,5},{5,9},{9,... | collective-permute-start | bytes 1572872 | tf_op jit(solution)/shard_map/ppermute | solution.py:14
  16.3 28.4 %collective-permute-start.3 = (bf16[2,256,512]{1,2,0:T(8,128)(2,1)S(1)}, bf16[2,256,512]{1,2,0:T(8,128)(2,1)S(1)}, u32[]{:S(2)}, u32[]{:S(2)}) collective-permute-start(bf16[2,256,512]{1,2,0:T(8,128)(2,1)S(1)} %pad_maximum_fusion.1), channel_id=1, source_target_pairs={{8,0},{12,4},{16,8},{20,12},{24,16},{28,20},{9,1},{13,5},{17,9},{2... | collective-permute-start | bytes 1572872 | tf_op jit(solution)/shard_map/ppermute | solution.py:14
  18.7 26.0 %collective-permute-start.2 = (bf16[2,256,512]{1,2,0:T(8,128)(2,1)S(1)}, bf16[2,256,512]{1,2,0:T(8,128)(2,1)S(1)}, u32[]{:S(2)}, u32[]{:S(2)}) collective-permute-start(bf16[2,256,512]{1,2,0:T(8,128)(2,1)S(1)} %pad_maximum_fusion.1), channel_id=1, source_target_pairs={{4,0},{8,4},{12,8},{16,12},{20,16},{24,20},{28,24},{5,1},{9,5},{13... | collective-permute-start | bytes 1572872 | tf_op jit(solution)/shard_map/ppermute | solution.py:14
  23.9 21.1 %copy-start.14 = (bf16[256,512]{0,1:T(8,128)(2,1)}, bf16[256,512]{0,1:T(8,128)(2,1)S(1)}, u32[]{:S(2)}) copy-start(bf16[256,512]{0,1:T(8,128)(2,1)S(1)} %copy.71) | copy-start | bytes 786436
  44.9 4.3 %copy-start.13 = (bf16[1,1280,512]{1,2,0:T(8,128)(2,1)}, bf16[1,1280,512]{1,2,0:T(8,128)(2,1)S(1)}, u32[]{:S(2)}) copy-start(bf16[1,1280,512]{1,2,0:T(8,128)(2,1)S(1)} %get-tuple-element.26) | copy-start | bytes 3932164
  44.9 8.2 %copy-start.12 = (bf16[1,1280,512]{1,2,0:T(8,128)(2,1)}, bf16[1,1280,512]{1,2,0:T(8,128)(2,1)S(1)}, u32[]{:S(2)}) copy-start(bf16[1,1280,512]{1,2,0:T(8,128)(2,1)S(1)} %get-tuple-element.27) | copy-start | bytes 3932164
  49.2 6.0 %copy-start.6 = (bf16[512,4096]{1,0:T(8,128)(2,1)S(1)}, bf16[512,4096]{1,0:T(8,128)(2,1)}, u32[]{:S(2)}) copy-start(bf16[512,4096]{1,0:T(8,128)(2,1)} %param.15) | copy-start | bytes 12582916
  53.2 1.5 copy-start.3
  58.0 130.5 %all-reduce.5.cloned.1.call-start = ((), (), s32[]{:S(2)}) async-start(), calls=%async_computation.3 | async-start | bytes 4194304 | tf_op jit(solution)/shard_map/psum | solution.py:131
  58.7 51.0 %copy-start = (bf16[256,4096]{1,0:T(8,128)(2,1)S(1)}, bf16[256,4096]{1,0:T(8,128)(2,1)}, u32[]{:S(2)}) copy-start(bf16[256,4096]{1,0:T(8,128)(2,1)} %param.14) | copy-start | bytes 6291460
  66.2 46.7 %copy-start.16 = (f32[4096]{0:T(1024)S(1)}, f32[4096]{0:T(1024)}, u32[]{:S(2)}) copy-start(f32[4096]{0:T(1024)} %param.16) | copy-start | bytes 49156
  109.7 2.4 copy-start.1
  114.0 7.3 %copy-start.11 = (f32[256,4096]{1,0:T(8,128)}, f32[256,4096]{1,0:T(8,128)S(1)}, u32[]{:S(2)}) copy-start(f32[256,4096]{1,0:T(8,128)S(1)} %broadcast_multiply_fusion) | copy-start | bytes 12582916
  114.0 8.2 %copy-start.17 = (f32[1024]{0:T(1024)S(1)}, f32[1024]{0:T(1024)}, u32[]{:S(2)}) copy-start(f32[1024]{0:T(1024)} %param.19) | copy-start | bytes 12292
  121.3 1.0 copy-start.18
  136.9 121.5 %reduce-scatter.2.cloned.1.call-start = ((), (), s32[]{:S(2)}) async-start(), calls=%async_computation.2 | async-start | bytes 2621440 | tf_op jit(solution)/shard_map/reduce_scatter | solution.py:109
  188.5 4.3 %copy-start.2 = (bf16[256,4096]{1,0:T(8,128)(2,1)S(1)}, bf16[256,4096]{1,0:T(8,128)(2,1)}, u32[]{:S(2)}) copy-start(bf16[256,4096]{1,0:T(8,128)(2,1)} %all-reduce.3.cloned.1.call-done) | copy-start | bytes 6291460
  188.5 4.3 %copy-start.9 = (bf16[256,4096]{1,0:T(8,128)(2,1)S(1)}, bf16[256,4096]{1,0:T(8,128)(2,1)}, u32[]{:S(2)}) copy-start(bf16[256,4096]{1,0:T(8,128)(2,1)} %param.21) | copy-start | bytes 6291460
  188.5 4.7 %copy-start.10 = (bf16[256,4096]{1,0:T(8,128)(2,1)S(1)}, bf16[256,4096]{1,0:T(8,128)(2,1)}, u32[]{:S(2)}) copy-start(bf16[256,4096]{1,0:T(8,128)(2,1)} %all-reduce.5.cloned.1.call-done) | copy-start | bytes 6291460
  193.2 4.4 %copy-start.7 = (bf16[512,4096]{1,0:T(8,128)(2,1)S(1)}, bf16[512,4096]{1,0:T(8,128)(2,1)}, u32[]{:S(2)}) copy-start(bf16[512,4096]{1,0:T(8,128)(2,1)} %param.15) | copy-start | bytes 12582916
  195.6 2.1 copy-start.5
  197.7 2.1 copy-start.4
  204.5 5.8 %copy-start.15 = (bf16[256,512]{0,1:T(8,128)(2,1)S(1)}, bf16[256,512]{0,1:T(8,128)(2,1)}, u32[]{:S(2)}) copy-start(bf16[256,512]{0,1:T(8,128)(2,1)} %copy-done.14) | copy-start | bytes 786436
  208.7 1.5 copy-start.8
  219.6 19.4 %collective-permute-start.4 = (bf16[2,256,512]{2,1,0:T(8,128)(2,1)}, bf16[2,256,512]{2,1,0:T(8,128)(2,1)}, u32[]{:S(2)}, u32[]{:S(2)}) collective-permute-start(bf16[2,256,512]{2,1,0:T(8,128)(2,1)} %get-tuple-element.22), channel_id=1, source_target_pairs={{8,0},{12,4},{16,8},{20,12},{24,16},{28,20},{9,1},{13,5},{17,9},{2... | collective-permute-start | bytes 1572872 | tf_op jit(solution)/shard_map/ppermute | solution.py:14
  222.0 16.9 %collective-permute-start.7 = (bf16[2,256,512]{2,1,0:T(8,128)(2,1)}, bf16[2,256,512]{2,1,0:T(8,128)(2,1)}, u32[]{:S(2)}, u32[]{:S(2)}) collective-permute-start(bf16[2,256,512]{2,1,0:T(8,128)(2,1)} %get-tuple-element.23), channel_id=1, source_target_pairs={{0,8},{4,12},{8,16},{12,20},{16,24},{20,28},{1,9},{5,13},{9,17},{1... | collective-permute-start | bytes 1572872 | tf_op jit(solution)/shard_map/ppermute | solution.py:14
  226.2 25.0 %collective-permute-start.6 = (bf16[2,256,512]{2,1,0:T(8,128)(2,1)}, bf16[2,256,512]{2,1,0:T(8,128)(2,1)}, u32[]{:S(2)}, u32[]{:S(2)}) collective-permute-start(bf16[2,256,512]{2,1,0:T(8,128)(2,1)} %get-tuple-element.24), channel_id=1, source_target_pairs={{0,4},{4,8},{8,12},{12,16},{16,20},{20,24},{24,28},{1,5},{5,9},{9,... | collective-permute-start | bytes 1572872 | tf_op jit(solution)/shard_map/ppermute | solution.py:14
  229.6 25.8 %collective-permute-start.5 = (bf16[2,256,512]{2,1,0:T(8,128)(2,1)}, bf16[2,256,512]{2,1,0:T(8,128)(2,1)}, u32[]{:S(2)}, u32[]{:S(2)}) collective-permute-start(bf16[2,256,512]{2,1,0:T(8,128)(2,1)} %get-tuple-element.25), channel_id=1, source_target_pairs={{4,0},{8,4},{12,8},{16,12},{20,16},{24,20},{28,24},{5,1},{9,5},{13... | collective-permute-start | bytes 1572872 | tf_op jit(solution)/shard_map/ppermute | solution.py:14
Sparse Core Ops, SparseCore 0:
  58.1 51.5 all-reduce.2
  137.0 51.4 all-reduce.4
  191.0 31.2 reduce-scatter.1
where the time goes:
time: 268 us; the launch traced here: 267 us
  waiting for transfers between devices  123 us (46%)
  matrix products  59 us (22%)
  starting transfers between devices  26.2 us (10%)
  other arithmetic  23 us (9%)
  local copies, waits for them, and re-layouts  21.9 us (8%)
  between operations  14.2 us (5%)
    psum x1, waiting for transfers between devices, shards(): lax.psum(head_part.astype(jnp.bfloat16), 'tp').astype(jnp.float32)  43.4 us
    psum x1, waiting for transfers between devices, shards(): lax.psum(back_part.astype(jnp.bfloat16), 'tp').astype(jnp.float32)  42.4 us
    ppermute x8, waiting for transfers between devices, from_behind(): return lax.ppermute(array, axis, pairs)  37.1 us
    ppermute x8, starting transfers between devices, from_behind(): return lax.ppermute(array, axis, pairs)  25.9 us
    unnamed x44, local copies, waits for them, and re-layouts  10.4 us
    dot_general x1, matrix products, shards(): jnp.dot(merged, down_source, preferred_element_type=jnp.float32)  9.1 us
    dot_general x1, matrix products, shards(): lax.dot_general(cotangent, down_source, (((1,), (1,)), ((), ())), preferr...  7.51 us
    dot_general x1, matrix products, shards(): lax.dot_general(grad_hidden, up_source, (((1,), (1,)), ((), ())), preferr...  7.32 us
  transfers between devices with their start and end apart: 11, of which 7 were waited for; matrix products, arithmetic and copies ran while one was open for 20% of the time, Pallas kernels for 0%

commit v1 on v0

--- a/solution.py
+++ b/solution.py
@@ -128,8 +128,8 @@
             grad_hidden, up_source, (((1,), (1,)), ((), ())), preferred_element_type=jnp.float32
         )
     )
-    grad_normed = cotangent.astype(jnp.float32) + lax.psum(
-        back_part.astype(jnp.bfloat16), "tp"
+    grad_normed = cotangent.astype(jnp.float32) + jnp.sum(
+        lax.all_gather(back_part.astype(jnp.bfloat16), "tp"), axis=0
     ).astype(jnp.float32)
     scaled = grad_normed * ln_gain
     grad_stream = (

time: 268 us -> 281 us (1.049)
  other arithmetic: 23 us -> 30.4 us
  waiting for transfers between devices: 123 us -> 128 us
    all_gather x0 -> x1, waiting for transfers between devices: none -> 49.3 us  [shards(): lax.all_gather(back_part.astype(jnp.bfloat16), 'tp')]
    psum x1 -> x0, waiting for transfers between devices: 42.4 us -> none  [shards(): lax.psum(back_part.astype(jnp.bfloat16), 'tp').astype(jnp.float32)]
    reduce_sum x0 -> x1, other arithmetic: none -> 6.94 us  [shards(): jnp.sum(lax.all_gather(back_part.astype(jnp.bfloat16), 'tp'), axis=0)]
  transfers between devices with their start and end apart: 11 -> 11, of which waited for: 7 -> 7; matrix products, arithmetic and copies ran while one was open for 20% -> 22% of each run, Pallas kernels for 0% -> 0%
where the time goes in v1:
time: 281 us; the launch traced here: 280 us
  waiting for transfers between devices  128 us (46%)
  matrix products  59.4 us (21%)
  other arithmetic  30.4 us (11%)
  starting transfers between devices  26.2 us (9%)
  local copies, waits for them, and re-layouts  22 us (8%)
  between operations  14.2 us (5%)
    all_gather x1, waiting for transfers between devices, shards(): lax.all_gather(back_part.astype(jnp.bfloat16), 'tp')  49.3 us
    psum x1, waiting for transfers between devices, shards(): lax.psum(head_part.astype(jnp.bfloat16), 'tp').astype(jnp.float32)  43.3 us
    ppermute x8, waiting for transfers between devices, from_behind(): return lax.ppermute(array, axis, pairs)  35.5 us
    ppermute x8, starting transfers between devices, from_behind(): return lax.ppermute(array, axis, pairs)  25.9 us
    unnamed x44, local copies, waits for them, and re-layouts  10.5 us
    dot_general x1, matrix products, shards(): jnp.dot(merged, down_source, preferred_element_type=jnp.float32)  9.11 us
    dot_general x1, matrix products, shards(): lax.dot_general(cotangent, down_source, (((1,), (1,)), ((), ())), preferr...  7.61 us
    dot_general x1, matrix products, shards(): lax.dot_general(grad_hidden, up_source, (((1,), (1,)), ((), ())), preferr...  7.36 us
  transfers between devices with their start and end apart: 11, of which 7 were waited for; matrix products, arithmetic and copies ran while one was open for 22% of the time, Pallas kernels for 0%

profile of v1, /device:TPU:16, one launch (start us, length us, event | category | flops | bytes accessed | tf_op | source)
XLA Modules:
  0.0 280.5 jit_solution(8071806295967051432)
XLA Ops:
  7.2 1.1 copy.47
  8.3 1.1 copy.48
  9.4 3.5 %collective-permute-start = (bf16[2,256,512]{1,2,0:T(8,128)(2,1)S(1)}, bf16[2,256,512]{1,2,0:T(8,128)(2,1)S(1)}, u32[]{:S(2)}, u32[]{:S(2)}) collective-permute-start(bf16[2,256,512]{1,2,0:T(8,128)(2,1)S(1)} %pad_maximum_fusion.1), channel_id=1, source_target_pairs={{0,8},{4,12},{8,16},{12,20},{16,24},{20,28},{1,9},{5,13},{9,17},{1... | collective-permute-start | bytes 1572872 | tf_op jit(solution)/shard_map/ppermute | solution.py:14
  12.9 3.4 %collective-permute-start.1 = (bf16[2,256,512]{1,2,0:T(8,128)(2,1)S(1)}, bf16[2,256,512]{1,2,0:T(8,128)(2,1)S(1)}, u32[]{:S(2)}, u32[]{:S(2)}) collective-permute-start(bf16[2,256,512]{1,2,0:T(8,128)(2,1)S(1)} %pad_maximum_fusion.1), channel_id=1, source_target_pairs={{0,4},{4,8},{8,12},{12,16},{16,20},{20,24},{24,28},{1,5},{5,9},{9,... | collective-permute-start | bytes 1572872 | tf_op jit(solution)/shard_map/ppermute | solution.py:14
  16.3 2.4 collective-permute-start.3
  18.7 3.3 %collective-permute-start.2 = (bf16[2,256,512]{1,2,0:T(8,128)(2,1)S(1)}, bf16[2,256,512]{1,2,0:T(8,128)(2,1)S(1)}, u32[]{:S(2)}, u32[]{:S(2)}) collective-permute-start(bf16[2,256,512]{1,2,0:T(8,128)(2,1)S(1)} %pad_maximum_fusion.1), channel_id=1, source_target_pairs={{4,0},{8,4},{12,8},{16,12},{20,16},{24,20},{28,24},{5,1},{9,5},{13... | collective-permute-start | bytes 1572872 | tf_op jit(solution)/shard_map/ppermute | solution.py:14
  22.8 1.1 copy.71
  23.9 1.1 collective-permute-done
  25.0 12.2 %collective-permute-done.1 = bf16[2,256,512]{1,2,0:T(8,128)(2,1)S(1)} collective-permute-done((bf16[2,256,512]{1,2,0:T(8,128)(2,1)S(1)}, bf16[2,256,512]{1,2,0:T(8,128)(2,1)S(1)}, u32[]{:S(2)}, u32[]{:S(2)}) %collective-permute-start.1) | collective-permute-done | bytes 524320 | tf_op jit(solution)/shard_map/ppermute | solution.py:14
  37.4 7.3 %collective-permute-done.2 = bf16[2,256,512]{1,2,0:T(8,128)(2,1)S(1)} collective-permute-done((bf16[2,256,512]{1,2,0:T(8,128)(2,1)S(1)}, bf16[2,256,512]{1,2,0:T(8,128)(2,1)S(1)}, u32[]{:S(2)}, u32[]{:S(2)}) %collective-permute-start.2) | collective-permute-done | bytes 524320 | tf_op jit(solution)/shard_map/ppermute | solution.py:14
  45.0 4.3 %exponential_reduce_fusion = (f32[4,256]{1,0:T(4,128)S(1)}, f32[4,256,1280]{1,2,0:T(8,128)}) fusion(bf16[1280,4,128]{0,2,1:T(8,128)(2,1)S(1)} %bitcast.58, bf16[256,4,128]{0,2,1:T(8,128)(2,1)S(1)} %bitcast.68, pred[1280]{0:T(1024)(128)(4,1)S(1)} %fusion.80), kind=kOutput, calls=%fused_computation.14 | convolution fusion | flops 340788480 | bytes 6821120 | tf_op jit(solution)/shard_map/sub | solution.py:70
  49.3 4.0 %fusion.20 = bf16[4,256,1280]{1,2,0:T(8,128)(2,1)S(1)} fusion(f32[4,256]{1,0:T(4,128)S(1)} %get-tuple-element.32, f32[4,256,1280]{1,2,0:T(8,128)} %get-tuple-element.33), kind=kLoop, calls=%fused_computation.40 | loop fusion | flops 2621440 | bytes 7868416 | tf_op jit(solution)/shard_map/convert_element_type | solution.py:72
  53.3 1.5 copy-done.3
  55.3 2.6 convolution_convert_fusion.2
  58.7 7.6 %convolution_multiply_fusion.1 = f32[256,1024]{1,0:T(8,128)} fusion(bf16[256,4096]{1,0:T(8,128)(2,1)} %param.21, bf16[1024,4096]{1,0:T(8,128)(2,1)} %param.18, f32[1024]{0:T(1024)S(1)} %get-tuple-element.30), kind=kOutput, calls=%fused_computation.50 | convolution fusion | flops 2147745792 | bytes 11538432 | tf_op jit(solution)/shard_map/dot_general | solution.py:119
  66.3 43.3 %all-reduce.2.cloned.1.call-done = bf16[256,4096]{1,0:T(8,128)(2,1)} async-done(((bf16[256,4096]{1,0:T(8,128)(2,1)}), bf16[256,4096]{1,0:T(8,128)(2,1)}) %all-reduce.2.cloned.1.call-update) | async-done | bytes 2097168 | tf_op jit(solution)/shard_map/psum | solution.py:78
  109.7 2.4 fusion.9
  113.0 1.0 broadcast_multiply_fusion
  114.0 7.2 %fusion.18 = f32[256,1024]{1,0:T(8,128)S(1)} fusion(bf16[4096,1024]{1,0:T(8,128)(2,1)} %param.17, f32[256,4096]{1,0:T(8,128)S(1)} %broadcast_multiply_fusion), kind=kOutput, calls=%fused_computation.37 | convolution fusion | flops 2148532224 | bytes 13631488 | tf_op jit(solution)/shard_map/dot_general | solution.py:103
  122.2 2.0 fusion.21
  124.2 5.5 %fusion.26 = bf16[256,1024]{1,0:T(8,128)(2,1)S(1)} fusion(s32[1024]{0:T(1024)S(1)} %broadcast_subtract_fusion, f32[256,1024]{1,0:T(8,128)} %convolution_multiply_fusion.1, f32[256,1024]{1,0:T(8,128)} %copy-done.18, f32[256,1024]{1,0:T(8,128)} %fusion.21, f32[1024]{0:T(1024)S(1)} %copy-done.17), kind=kOutput, calls=%fused_computation.51 | convolution fusion | flops 1086586880 | bytes 3678208 | tf_op jit(solution)/shard_map/dot_general | solution.py:96
  129.7 7.4 %convolution_convert_fusion = bf16[256,4096]{1,0:T(8,128)(2,1)} fusion(bf16[256,1024]{1,0:T(8,128)(2,1)S(1)} %fusion.26, bf16[4096,1024]{1,0:T(8,128)(2,1)} %param.17), kind=kOutput, calls=%fused_computation.10 | convolution fusion | flops 2148532224 | bytes 11010048 | tf_op jit(solution)/shard_map/dot_general | solution.py:127
  137.1 9.1 %convolution_convert_fusion.1 = bf16[256,4096]{1,0:T(8,128)(2,1)} fusion(bf16[1024,4096]{1,0:T(8,128)(2,1)} %param.18, s32[1024]{0:T(1024)S(1)} %broadcast_subtract_fusion, f32[256,1024]{1,0:T(8,128)} %copy-done.18, f32[256,1024]{1,0:T(8,128)} %fusion.21, f32[1024]{0:T(1024)S(1)} %get-tuple-element.31), kind=kOutput, calls=%fused_computation.11 | convolution fusion | flops 2691694592 | bytes 12591104 | tf_op jit(solution)/shard_map/dot_general | solution.py:110
  146.3 49.3 %all-gather.3.cloned.1.call-done = bf16[1024,4096]{1,0:T(8,128)(2,1)} async-done(((bf16[256,4096]{1,0:T(8,128)(2,1)}), bf16[1024,4096]{1,0:T(8,128)(2,1)}) %all-gather.3.cloned.1.call-update) | async-done | bytes 8388624 | tf_op jit(solution)/shard_map/all_gather | solution.py:132
  195.6 6.9 %reduce_sum.79 = bf16[256,4096]{1,0:T(8,128)(2,1)} reduce(bf16[4,256,4096]{2,1,0:T(8,128)(2,1)} %bitcast.55, bf16[]{:T(256)} %constant.70.clone.1), dimensions={0}, to_apply=%region_7.8 | reduce | flops 3145728 | bytes 10485762 | tf_op jit(solution)/shard_map/reduce_sum | solution.py:131
  202.5 4.8 %fusion.11 = (f32[256]{0:T(256)S(1)}, f32[256]{0:T(256)S(1)}) fusion(bf16[256,4096]{1,0:T(8,128)(2,1)} %reduce_sum.79, bf16[256,4096]{1,0:T(8,128)(2,1)} %param.21, f32[4096]{0:T(1024)S(1)} %copy-done.16, f32[256]{0:T(256)S(1)} %add_sqrt_fusion, f32[256]{0:T(256)S(1)} %broadcast_multiply_fusion.3, bf16[256,4096]{1,0:T(8,128)(2,1)} %all-reduce.2.cloned.1.call-done, ...), kind=kLoop, calls=%fused_computation.30 | loop fusion | flops 12582400 | bytes 8409088 | tf_op jit(solution)/shard_map/reduce_sum | solution.py:137
  208.3 2.4 subtract_divide_fusion
  210.6 1.9 copy-done.5
  212.6 1.3 fusion.30
  214.3 2.5 fusion.100
  216.8 2.1 copy.61
  219.1 4.3 %multiply_convert_fusion = bf16[4,256,1280]{1,2,0:T(8,128)(2,1)S(1)} fusion(bf16[256,4,128]{0,2,1:T(8,128)(2,1)S(1)} %bitcast.66, bf16[1280,4,128]{0,2,1:T(8,128)(2,1)} %bitcast.57, f32[4,256]{1,0:T(4,128)S(1)} %bitcast.70, f32[4,256]{1,0:T(4,128)S(1)} %get-tuple-element.32, f32[4,256,1280]{1,2,0:T(8,128)} %get-tuple-element.33), kind=kOutput, calls=%fused_computation.8 | convolution fusion | flops 340787200 | bytes 9445376 | tf_op jit(solution)/shard_map/rhd,khd->hrk/dot_general | solution.py:151
  223.4 1.6 copy-done.9
  224.9 2.5 convolution_multiply_fusion
  227.4 3.3 %copy.60 = f32[1,1280,512]{2,1,0:T(8,128)} copy(f32[1,1280,512]{1,2,0:T(8,128)} %bitcast.54) | data formatting | bytes 5242880 | tf_op jit(solution)/shard_map/stack;reshape | solution.py:165
  230.6 2.2 fusion.2
  232.8 1.4 fusion.98
  234.2 2.4 collective-permute-start.4
  236.6 4.2 %collective-permute-start.7 = (bf16[2,256,512]{2,1,0:T(8,128)(2,1)}, bf16[2,256,512]{2,1,0:T(8,128)(2,1)}, u32[]{:S(2)}, u32[]{:S(2)}) collective-permute-start(bf16[2,256,512]{2,1,0:T(8,128)(2,1)} %get-tuple-element.23), channel_id=1, source_target_pairs={{0,8},{4,12},{8,16},{12,20},{16,24},{20,28},{1,9},{5,13},{9,17},{1... | collective-permute-start | bytes 1572872 | tf_op jit(solution)/shard_map/ppermute | solution.py:14
  240.8 3.4 %collective-permute-start.6 = (bf16[2,256,512]{2,1,0:T(8,128)(2,1)}, bf16[2,256,512]{2,1,0:T(8,128)(2,1)}, u32[]{:S(2)}, u32[]{:S(2)}) collective-permute-start(bf16[2,256,512]{2,1,0:T(8,128)(2,1)} %get-tuple-element.24), channel_id=1, source_target_pairs={{0,4},{4,8},{8,12},{12,16},{16,20},{20,24},{24,28},{1,5},{5,9},{9,... | collective-permute-start | bytes 1572872 | tf_op jit(solution)/shard_map/ppermute | solution.py:14
  244.2 3.4 %collective-permute-start.5 = (bf16[2,256,512]{2,1,0:T(8,128)(2,1)}, bf16[2,256,512]{2,1,0:T(8,128)(2,1)}, u32[]{:S(2)}, u32[]{:S(2)}) collective-permute-start(bf16[2,256,512]{2,1,0:T(8,128)(2,1)} %get-tuple-element.25), channel_id=1, source_target_pairs={{4,0},{8,4},{12,8},{16,12},{20,16},{24,20},{28,24},{5,1},{9,5},{13... | collective-permute-start | bytes 1572872 | tf_op jit(solution)/shard_map/ppermute | solution.py:14
  247.6 2.5 convert_add_fusion.1
  250.1 2.7 convolution_multiply_fusion.2
  253.7 2.3 constant_dynamic-slice_fusion
  256.0 10.7 %collective-permute-done.6 = bf16[2,256,512]{2,1,0:T(8,128)(2,1)} collective-permute-done((bf16[2,256,512]{2,1,0:T(8,128)(2,1)}, bf16[2,256,512]{2,1,0:T(8,128)(2,1)}, u32[]{:S(2)}, u32[]{:S(2)}) %collective-permute-start.6) | collective-permute-done | bytes 524320 | tf_op jit(solution)/shard_map/ppermute | solution.py:14
  266.7 4.1 %collective-permute-done.5 = bf16[2,256,512]{2,1,0:T(8,128)(2,1)} collective-permute-done((bf16[2,256,512]{2,1,0:T(8,128)(2,1)}, bf16[2,256,512]{2,1,0:T(8,128)(2,1)}, u32[]{:S(2)}, u32[]{:S(2)}) %collective-permute-start.5) | collective-permute-done | bytes 524320 | tf_op jit(solution)/shard_map/ppermute | solution.py:14
  270.9 2.0 fusion.50
  272.9 1.0 slice_bitcast_fusion
  (64 shorter events, 7.0 us)
Async XLA Ops:
  7.2 102.5 %all-reduce.2.cloned.1.call-start = ((), (), s32[]{:S(2)}) async-start(), calls=%async_computation.1 | async-start | bytes 4194304 | tf_op jit(solution)/shard_map/psum | solution.py:78
  9.4 15.6 %collective-permute-start = (bf16[2,256,512]{1,2,0:T(8,128)(2,1)S(1)}, bf16[2,256,512]{1,2,0:T(8,128)(2,1)S(1)}, u32[]{:S(2)}, u32[]{:S(2)}) collective-permute-start(bf16[2,256,512]{1,2,0:T(8,128)(2,1)S(1)} %pad_maximum_fusion.1), channel_id=1, source_target_pairs={{0,8},{4,12},{8,16},{12,20},{16,24},{20,28},{1,9},{5,13},{9,17},{1... | collective-permute-start | bytes 1572872 | tf_op jit(solution)/shard_map/ppermute | solution.py:14
  12.9 24.3 %collective-permute-start.1 = (bf16[2,256,512]{1,2,0:T(8,128)(2,1)S(1)}, bf16[2,256,512]{1,2,0:T(8,128)(2,1)S(1)}, u32[]{:S(2)}, u32[]{:S(2)}) collective-permute-start(bf16[2,256,512]{1,2,0:T(8,128)(2,1)S(1)} %pad_maximum_fusion.1), channel_id=1, source_target_pairs={{0,4},{4,8},{8,12},{12,16},{16,20},{20,24},{24,28},{1,5},{5,9},{9,... | collective-permute-start | bytes 1572872 | tf_op jit(solution)/shard_map/ppermute | solution.py:14
  16.3 28.4 %collective-permute-start.3 = (bf16[2,256,512]{1,2,0:T(8,128)(2,1)S(1)}, bf16[2,256,512]{1,2,0:T(8,128)(2,1)S(1)}, u32[]{:S(2)}, u32[]{:S(2)}) collective-permute-start(bf16[2,256,512]{1,2,0:T(8,128)(2,1)S(1)} %pad_maximum_fusion.1), channel_id=1, source_target_pairs={{8,0},{12,4},{16,8},{20,12},{24,16},{28,20},{9,1},{13,5},{17,9},{2... | collective-permute-start | bytes 1572872 | tf_op jit(solution)/shard_map/ppermute | solution.py:14
  18.7 26.0 %collective-permute-start.2 = (bf16[2,256,512]{1,2,0:T(8,128)(2,1)S(1)}, bf16[2,256,512]{1,2,0:T(8,128)(2,1)S(1)}, u32[]{:S(2)}, u32[]{:S(2)}) collective-permute-start(bf16[2,256,512]{1,2,0:T(8,128)(2,1)S(1)} %pad_maximum_fusion.1), channel_id=1, source_target_pairs={{4,0},{8,4},{12,8},{16,12},{20,16},{24,20},{28,24},{5,1},{9,5},{13... | collective-permute-start | bytes 1572872 | tf_op jit(solution)/shard_map/ppermute | solution.py:14
  23.9 21.1 %copy-start.14 = (bf16[256,512]{0,1:T(8,128)(2,1)}, bf16[256,512]{0,1:T(8,128)(2,1)S(1)}, u32[]{:S(2)}) copy-start(bf16[256,512]{0,1:T(8,128)(2,1)S(1)} %copy.71) | copy-start | bytes 786436
  44.9 4.4 %copy-start.13 = (bf16[1,1280,512]{1,2,0:T(8,128)(2,1)}, bf16[1,1280,512]{1,2,0:T(8,128)(2,1)S(1)}, u32[]{:S(2)}) copy-start(bf16[1,1280,512]{1,2,0:T(8,128)(2,1)S(1)} %get-tuple-element.26) | copy-start | bytes 3932164
  44.9 8.3 %copy-start.12 = (bf16[1,1280,512]{1,2,0:T(8,128)(2,1)}, bf16[1,1280,512]{1,2,0:T(8,128)(2,1)S(1)}, u32[]{:S(2)}) copy-start(bf16[1,1280,512]{1,2,0:T(8,128)(2,1)S(1)} %get-tuple-element.27) | copy-start | bytes 3932164
  49.3 6.0 %copy-start.7 = (bf16[512,4096]{1,0:T(8,128)(2,1)S(1)}, bf16[512,4096]{1,0:T(8,128)(2,1)}, u32[]{:S(2)}) copy-start(bf16[512,4096]{1,0:T(8,128)(2,1)} %param.15) | copy-start | bytes 12582916
  53.3 1.5 copy-start.3
  58.0 137.6 %all-gather.3.cloned.1.call-start = ((), (), s32[]{:S(2)}) async-start(), calls=%async_computation.3 | async-start | bytes 10485760 | tf_op jit(solution)/shard_map/all_gather | solution.py:132
  58.7 51.0 %copy-start = (bf16[256,4096]{1,0:T(8,128)(2,1)S(1)}, bf16[256,4096]{1,0:T(8,128)(2,1)}, u32[]{:S(2)}) copy-start(bf16[256,4096]{1,0:T(8,128)(2,1)} %param.14) | copy-start | bytes 6291460
  66.3 46.6 %copy-start.16 = (f32[4096]{0:T(1024)S(1)}, f32[4096]{0:T(1024)}, u32[]{:S(2)}) copy-start(f32[4096]{0:T(1024)} %param.16) | copy-start | bytes 49156
  109.7 2.4 copy-start.1
  114.0 7.3 %copy-start.11 = (f32[256,4096]{1,0:T(8,128)}, f32[256,4096]{1,0:T(8,128)S(1)}, u32[]{:S(2)}) copy-start(f32[256,4096]{1,0:T(8,128)S(1)} %broadcast_multiply_fusion) | copy-start | bytes 12582916
  114.0 8.2 %copy-start.17 = (f32[1024]{0:T(1024)S(1)}, f32[1024]{0:T(1024)}, u32[]{:S(2)}) copy-start(f32[1024]{0:T(1024)} %param.19) | copy-start | bytes 12292
  121.3 1.0 copy-start.18
  137.1 110.5 %reduce-scatter.2.cloned.1.call-start = ((), (), s32[]{:S(2)}) async-start(), calls=%async_computation.2 | async-start | bytes 2621440 | tf_op jit(solution)/shard_map/reduce_scatter | solution.py:109
  202.5 4.8 %copy-start.2 = (bf16[256,4096]{1,0:T(8,128)(2,1)S(1)}, bf16[256,4096]{1,0:T(8,128)(2,1)}, u32[]{:S(2)}) copy-start(bf16[256,4096]{1,0:T(8,128)(2,1)} %all-reduce.2.cloned.1.call-done) | copy-start | bytes 6291460
  202.5 5.0 %copy-start.6 = (bf16[256,4096]{1,0:T(8,128)(2,1)S(1)}, bf16[256,4096]{1,0:T(8,128)(2,1)}, u32[]{:S(2)}) copy-start(bf16[256,4096]{1,0:T(8,128)(2,1)} %reduce_sum.79) | copy-start | bytes 6291460
  202.5 5.7 %copy-start.10 = (bf16[256,4096]{1,0:T(8,128)(2,1)S(1)}, bf16[256,4096]{1,0:T(8,128)(2,1)}, u32[]{:S(2)}) copy-start(bf16[256,4096]{1,0:T(8,128)(2,1)} %param.21) | copy-start | bytes 6291460
  208.2 4.3 %copy-start.8 = (bf16[512,4096]{1,0:T(8,128)(2,1)S(1)}, bf16[512,4096]{1,0:T(8,128)(2,1)}, u32[]{:S(2)}) copy-start(bf16[512,4096]{1,0:T(8,128)(2,1)} %param.15) | copy-start | bytes 12582916
  210.6 1.9 copy-start.5
  212.6 1.7 copy-start.4
  219.1 5.8 %copy-start.15 = (bf16[256,512]{0,1:T(8,128)(2,1)S(1)}, bf16[256,512]{0,1:T(8,128)(2,1)}, u32[]{:S(2)}) copy-start(bf16[256,512]{0,1:T(8,128)(2,1)} %copy-done.14) | copy-start | bytes 786436
  223.3 1.6 copy-start.9
  234.2 21.8 %collective-permute-start.4 = (bf16[2,256,512]{2,1,0:T(8,128)(2,1)}, bf16[2,256,512]{2,1,0:T(8,128)(2,1)}, u32[]{:S(2)}, u32[]{:S(2)}) collective-permute-start(bf16[2,256,512]{2,1,0:T(8,128)(2,1)} %get-tuple-element.22), channel_id=1, source_target_pairs={{8,0},{12,4},{16,8},{20,12},{24,16},{28,20},{9,1},{13,5},{17,9},{2... | collective-permute-start | bytes 1572872 | tf_op jit(solution)/shard_map/ppermute | solution.py:14
  236.6 19.4 %collective-permute-start.7 = (bf16[2,256,512]{2,1,0:T(8,128)(2,1)}, bf16[2,256,512]{2,1,0:T(8,128)(2,1)}, u32[]{:S(2)}, u32[]{:S(2)}) collective-permute-start(bf16[2,256,512]{2,1,0:T(8,128)(2,1)} %get-tuple-element.23), channel_id=1, source_target_pairs={{0,8},{4,12},{8,16},{12,20},{16,24},{20,28},{1,9},{5,13},{9,17},{1... | collective-permute-start | bytes 1572872 | tf_op jit(solution)/shard_map/ppermute | solution.py:14
  240.8 25.9 %collective-permute-start.6 = (bf16[2,256,512]{2,1,0:T(8,128)(2,1)}, bf16[2,256,512]{2,1,0:T(8,128)(2,1)}, u32[]{:S(2)}, u32[]{:S(2)}) collective-permute-start(bf16[2,256,512]{2,1,0:T(8,128)(2,1)} %get-tuple-element.24), channel_id=1, source_target_pairs={{0,4},{4,8},{8,12},{12,16},{16,20},{20,24},{24,28},{1,5},{5,9},{9,... | collective-permute-start | bytes 1572872 | tf_op jit(solution)/shard_map/ppermute | solution.py:14
  244.2 26.7 %collective-permute-start.5 = (bf16[2,256,512]{2,1,0:T(8,128)(2,1)}, bf16[2,256,512]{2,1,0:T(8,128)(2,1)}, u32[]{:S(2)}, u32[]{:S(2)}) collective-permute-start(bf16[2,256,512]{2,1,0:T(8,128)(2,1)} %get-tuple-element.25), channel_id=1, source_target_pairs={{4,0},{8,4},{12,8},{16,12},{20,16},{24,20},{28,24},{5,1},{9,5},{13... | collective-permute-start | bytes 1572872 | tf_op jit(solution)/shard_map/ppermute | solution.py:14
Sparse Core Ops, SparseCore 0:
  58.1 51.5 all-reduce.1
  137.2 58.3 all-gather.2
  198.1 31.1 reduce-scatter.1
